TPU v7x, 768 devices: a whole 4x8x12 slice. The times are simulated.
768 devices in a mesh: dp: 8 (over y), tensor: 96 (over z, x, core).
Axes of the slice: x: 4, y: 8, z: 12, core: 2. Of those that a mesh axis runs over, the one named last changes fastest.
Arguments:
- grad_out: bfloat16 [1536, 8192], P('dp'), may hold values from -6 to 6
- gate_act: bfloat16 [1536, 16896], P('dp', 'tensor'), may hold values from -20 to 20
- up_act: bfloat16 [1536, 16896], P('dp', 'tensor'), may hold values from -6 to 6
- w_gate: bfloat16 [16896, 8192], P('tensor'), may hold values from -0.0625 to 0.0625
- w_up: bfloat16 [16896, 8192], P('tensor'), may hold values from -0.0625 to 0.0625
- w_down: bfloat16 [16896, 8192], P('tensor'), may hold values from -0.046875 to 0.046875
Outputs:
- input_grad: bfloat16 [1536, 8192], P(('dp', 'tensor'))
- down_grad: bfloat16 [16896, 8192], P('tensor', 'dp')
All inputs are finite; a program needn't handle non-finite values.
Results may differ from a plain program's by a relative error of at most 0.014.
Values may be sent and summed in bfloat16 or wider, within the bound.
No kernel may reach another device: no remote copies, remote signals or barrier semaphores. Data moves between devices by JAX's collectives and lax.ppermute only.
A program may use at most 64 MiB of HBM per device.

v0:
```python
import jax
import jax.numpy as jnp
from jax import lax
from jax.sharding import PartitionSpec as P


def local(grad_out, gate_act, up_act, w_gate, w_up, w_down):
    gate = gate_act.astype(jnp.float32)
    up = up_act.astype(jnp.float32)
    sig = jax.nn.sigmoid(gate)
    silu = gate * sig
    hidden = (silu * up).astype(jnp.bfloat16)
    hidden_grad = lax.dot_general(
        grad_out, w_down, (((1,), (1,)), ((), ())), preferred_element_type=jnp.float32
    )
    gate_grad = (hidden_grad * up * sig * (1.0 + gate * (1.0 - sig))).astype(jnp.bfloat16)
    up_grad = (hidden_grad * silu).astype(jnp.bfloat16)
    full_terms = jnp.dot(gate_grad, w_gate, preferred_element_type=jnp.float32) + jnp.dot(
        up_grad, w_up, preferred_element_type=jnp.float32
    )
    summed = lax.psum_scatter(full_terms, "tensor", scatter_dimension=0, tiled=True)
    input_grad = summed.astype(jnp.bfloat16)
    partial_sum = lax.dot_general(
        hidden, grad_out, (((0,), (0,)), ((), ())), preferred_element_type=jnp.float32
    )
    down_grad = lax.psum_scatter(
        partial_sum.astype(jnp.bfloat16), "dp", scatter_dimension=1, tiled=True
    )
    return (input_grad, down_grad)


def solution(mesh):
    placed = (
        P("dp", None),
        P("dp", "tensor"),
        P("dp", "tensor"),
        P("tensor", None),
        P("tensor", None),
        P("tensor", None),
    )
    return jax.shard_map(
        local,
        mesh=mesh,
        in_specs=placed,
        out_specs=(P(("dp", "tensor"), None), P("tensor", "dp")),
        check_vma=False,
    )
```

profile of v0, /device:TPU:32, one launch (start us, length us, event | category | flops | bytes accessed | tf_op | source)
XLA Modules:
  0.0 480.8 jit_solution(876936034588708818)
XLA Ops:
  7.2 0.0 copy-start
  7.2 0.0 reduce-scatter.2.cloned.1.call-start
  7.2 1.8 copy-done
  9.1 3.4 convolution_convert_fusion
  12.5 0.0 reduce-scatter.2.cloned.1.call-update
  12.5 0.0 copy-start.2
  12.5 0.0 copy-start.3
  12.5 0.0 copy-start.4
  12.5 3.0 fusion.15
  15.5 0.0 copy-done.2
  15.5 0.0 copy-done.3
  15.5 0.0 copy-done.4
  15.5 0.0 copy-start.1
  15.5 1.1 fusion.9
  16.6 0.7 copy-done.1
  17.3 3.7 convolution_add_fusion
  21.0 1.3 dynamic-slice
  22.9 449.5 %all-reduce.2 = bf16[192,8192]{1,0:T(8,128)(2,1)} all-reduce(f32[192,8192]{1,0:T(8,128)} %convolution_add_fusion), channel_id=2, replica_groups=mesh['dp'=8,'tensor'=96] {'tensor'}, use_global_device_ids=true, to_apply=%region_0.0.clone | all-reduce | flops 1572864 | bytes 9437184
  472.4 1.6 dynamic-slice_convert_fusion
  474.0 0.0 reduce-scatter.2.cloned.1.call-done
Async XLA Ops:
  7.2 1.9 copy-start
  7.2 466.8 %reduce-scatter.2.cloned.1.call-start = ((), (), s32[]{:S(2)}) async-start(), calls=%async_computation.1 | async-start | bytes 3244032 | tf_op jit(solution)/shard_map/reduce_scatter | solution.py:26
  12.5 3.0 copy-start.2
  12.5 3.0 copy-start.3
  12.5 3.0 copy-start.4
  15.5 1.8 copy-start.1
Sparse Core Ops, SparseCore 0:
  12.6 55.3 reduce-scatter.1
where the time goes:
time: 481 us
  blocking collectives  449 us (93%)
  between operations  14.8 us (3%)
  matrix products  11.1 us (2%)
  local copies, waits for them, and re-layouts  5.43 us (1%)
    unnamed x1, blocking collectives  449 us
  transfers between devices with their start and end apart: 1, of which 0 were waited for; matrix products, arithmetic and copies ran while one was open for 2% of the time, Pallas kernels for 0%

commit v1 on v0

v1 whole, which is shorter than its diff:
```python
import jax
import jax.numpy as jnp
from jax import lax
from jax.experimental import pallas as pl
from jax.experimental.pallas import tpu as pltpu
from jax.sharding import Mesh, PartitionSpec as P

NY, NZ, NX, NC = 8, 12, 4, 2
PLANE = ("z", "x", "c")
PIECES = 4
CHUNKS = 4
f32, bf16 = jnp.float32, jnp.bfloat16


def shift(n, d):
    return [(i, (i + d) % n) for i in range(n)]


def dot(a, b, over):
    return lax.dot_general(a, b, (over, ((), ())), preferred_element_type=f32)


def one_hot(order):
    n = order.shape[0]
    cols = lax.broadcasted_iota(jnp.int32, (n, n), 1)
    return jnp.where(cols == order, 1.0, 0.0).astype(bf16)


def pack_kernel(at_ref, order_ref, grad_ref, gate_ref, up_ref, out_ref):
    ny, _, width = out_ref.shape
    share = grad_ref.shape[0]
    ff = gate_ref.shape[0]
    tokens = gate_ref.shape[1]
    gate = gate_ref[...].astype(f32)
    hidden = (gate * jax.nn.sigmoid(gate) * up_ref[...].astype(f32)).astype(bf16)
    hidden = dot(one_hot(order_ref[...]), hidden, ((1,), (1,))).astype(bf16)
    hidden = jnp.concatenate([hidden, jnp.zeros((tokens, width - ff), bf16)], axis=1)
    for y in range(ny):
        for b in range(PIECES):
            start = (y * PIECES + b) * width
            out_ref[y, b * share : (b + 1) * share, :] = grad_ref[
                :, start : start + width
            ]
        out_ref[y, PIECES * share :, :] = hidden


def main_kernel(
    order_ref, gate_ref, up_ref, grad_hbm, wd_hbm, wg_hbm, wu_hbm,
    theirs_ref, ours_ref, grad, wd, w, grad_sem, wd_sem, wg_sem, wu_sem,
):
    ff, d = wd.shape
    half = ours_ref.shape[0]
    step = d // CHUNKS
    chunks = [pl.ds(i * step, step) for i in range(CHUNKS)]
    copies = []
    for i, c in enumerate(chunks):
        copies.append(
            (
                pltpu.make_async_copy(grad_hbm.at[:, c], grad.at[:, c], grad_sem.at[i]),
                pltpu.make_async_copy(wd_hbm.at[:, c], wd.at[:, c], wd_sem.at[i]),
            )
        )
    weights = []
    for i, c in enumerate(chunks):
        weights.append(
            (
                pltpu.make_async_copy(wg_hbm.at[:, c], w.at[:ff, c], wg_sem.at[i]),
                pltpu.make_async_copy(wu_hbm.at[:, c], w.at[ff:, c], wu_sem.at[i]),
            )
        )
    for pair in copies + weights:
        for copy in pair:
            copy.start()

    gate = gate_ref[...].astype(f32)
    up = up_ref[...].astype(f32)
    sig = jax.nn.sigmoid(gate)
    silu = gate * sig
    slope = up * sig * (1.0 + gate * (1.0 - sig))
    pick = one_hot(order_ref[...])

    hidden_grad = jnp.zeros(gate.shape, f32)
    for pair, c in zip(copies, chunks):
        for copy in pair:
            copy.wait()
        hidden_grad = hidden_grad + dot(wd[:, c], grad[:, c], ((1,), (1,)))
    both = jnp.concatenate(
        [(hidden_grad * slope).astype(bf16), (hidden_grad * silu).astype(bf16)], axis=0
    )
    both = dot(pick, both, ((1,), (1,))).astype(bf16)
    for i, pair in enumerate(weights):
        for copy in pair:
            copy.wait()

        def body(n, carry, i=i):
            at = pl.ds(pl.multiple_of(i * step + n * 512, 512), 512)
            part = dot(both, w[:, at], ((1,), (0,))).astype(bf16)
            ours_ref[:, at] = part[:half]
            theirs_ref[:, at] = part[half:]
            return carry

        lax.fori_loop(0, step // 512, body, 0)


def down_kernel(own_ref, x1_ref, x2_ref, x3_ref, core_ref, out_ref, h, g):
    ny, _, width = own_ref.shape
    ff = out_ref.shape[0]
    share = x1_ref.shape[1] // PIECES
    block = ny * share
    for j in range(NC):
        for k in range(NX):
            jk = j * NX + k
            at = PIECES * share + jk * share
            h[jk * block : (jk + 1) * block, :] = own_ref[:, at : at + share, :].reshape(
                block, width
            )
            for b in range(PIECES):
                rows_b = slice(b * share, (b + 1) * share)
                if j == 1:
                    piece = core_ref[k, :, rows_b, :]
                else:
                    piece = (own_ref, x1_ref, x2_ref, x3_ref)[k][:, rows_b, :]
                g[jk * block : (jk + 1) * block, b * width : (b + 1) * width] = (
                    piece.reshape(block, width)
                )
    left = h[...]
    for b in range(PIECES):
        c = slice(b * width, (b + 1) * width)
        out_ref[:, c] = dot(left, g[:, c], ((0,), (0,)))[:ff].astype(bf16)


VMEM = pl.BlockSpec(memory_space=pltpu.VMEM)
ANY = pl.BlockSpec(memory_space=pl.ANY)


def local(grad_out, gate_act, up_act, w_gate, w_up, w_down):
    tokens, d = grad_out.shape
    ff = gate_act.shape[1]
    share = tokens // (NX * NC)
    cols = d // NY
    width = cols // PIECES
    per = tokens // (NZ * NX * NC)
    half = tokens // NC
    xi, ci = lax.axis_index("x"), lax.axis_index("c")
    gate_t, up_t = gate_act.T, up_act.T

    i = lax.iota(jnp.int32, tokens)
    j, k, t = i // (NX * share), (i // share) % NX, i % share
    by_share = (((xi + k) % NX) * NC + (ci + j) % NC) * share + t
    k, z, r = (i // (NZ * per)) % NX, (i // per) % NZ, i % per
    j = i // half
    by_owner = ((z * NX + (xi + k) % NX) * NC + (ci + j) % NC) * per + r

    packed = pl.pallas_call(
        pack_kernel,
        name="pack",
        grid_spec=pltpu.PrefetchScalarGridSpec(
            num_scalar_prefetch=1,
            grid=(1,),
            in_specs=[
                pl.BlockSpec((tokens, 1), lambda g, at: (0, 0)),
                pl.BlockSpec((share, d), lambda g, at: (at[0], 0)),
                pl.BlockSpec((ff, tokens), lambda g, at: (0, 0)),
                pl.BlockSpec((ff, tokens), lambda g, at: (0, 0)),
            ],
            out_specs=pl.BlockSpec(
                (NY, PIECES * share + tokens, width), lambda g, at: (0, 0, 0)
            ),
        ),
        out_shape=jax.ShapeDtypeStruct((NY, PIECES * share + tokens, width), bf16),
        cost_estimate=pl.CostEstimate(
            flops=2 * tokens * tokens * ff, bytes_accessed=2_000_000, transcendentals=0
        ),
    )((xi * NC + ci)[None], by_share[:, None], grad_out, gate_t, up_t)
    packed = lax.all_to_all(packed, "y", 0, 0)

    theirs, ours = pl.pallas_call(
        main_kernel,
        name="main",
        in_specs=[VMEM, VMEM, VMEM, ANY, ANY, ANY, ANY],
        out_specs=[VMEM, VMEM],
        out_shape=[jax.ShapeDtypeStruct((half, d), bf16)] * 2,
        scratch_shapes=[
            pltpu.VMEM((tokens, d), bf16),
            pltpu.VMEM((ff, d), bf16),
            pltpu.VMEM((2 * ff, d), bf16),
        ]
        + [pltpu.SemaphoreType.DMA((CHUNKS,))] * 4,
        cost_estimate=pl.CostEstimate(
            flops=6 * tokens * ff * d, bytes_accessed=14_000_000, transcendentals=0
        ),
    )(by_owner[:, None], gate_t, up_t, grad_out, w_down, w_gate, w_up)
    theirs = lax.ppermute(theirs, "c", shift(NC, 1))
    total = ours.astype(f32) + theirs.astype(f32)
    blk = half // NX
    own = total[:blk]
    sent = total[blk:].astype(bf16)
    got = [
        lax.ppermute(sent[(k - 1) * blk : k * blk], "x", shift(NX, k))
        for k in (1, 3, 2)
    ]
    own = own + sum(a.astype(f32) for a in got)
    parts = lax.all_to_all(own.astype(bf16).reshape(NZ, per, d), "z", 0, 0)
    input_grad = jnp.sum(parts.astype(f32), axis=0).astype(bf16)

    g0 = packed[:, : PIECES * share, :]
    g = [lax.ppermute(g0, "x", shift(NX, -k)) for k in range(1, NX)]
    other = lax.ppermute(jnp.stack([g0] + g), "c", shift(NC, 1))
    down_grad = pl.pallas_call(
        down_kernel,
        name="down",
        in_specs=[VMEM] * 5,
        out_specs=VMEM,
        out_shape=jax.ShapeDtypeStruct((ff, cols), bf16),
        scratch_shapes=[
            pltpu.VMEM((NY * tokens, width), bf16),
            pltpu.VMEM((NY * tokens, cols), bf16),
        ],
        cost_estimate=pl.CostEstimate(
            flops=2 * NY * tokens * ff * cols, bytes_accessed=8_000_000, transcendentals=0
        ),
    )(packed, *g, other)
    return (input_grad, down_grad)


def solution(mesh):
    mesh4 = Mesh(mesh.devices.reshape(NY, NZ, NX, NC), ("y",) + PLANE)
    placed = (
        P("y", None),
        P("y", PLANE),
        P("y", PLANE),
        P(PLANE, None),
        P(PLANE, None),
        P(PLANE, None),
    )
    return jax.shard_map(
        local,
        mesh=mesh4,
        in_specs=placed,
        out_specs=(P(("y",) + PLANE, None), P(PLANE, "y")),
        check_vma=False,
    )
```

time: 481 us -> 143 us (0.30)
  the two profiles are of different devices: /device:TPU:32 before, /device:TPU:4 now
where the time goes in v1:
time: 143 us; the launch traced here: 142 us
  waiting for transfers between devices  45.9 us (32%)
  starting transfers between devices  33.2 us (23%)
  blocking collectives  32.2 us (23%)
  Pallas kernels  18.3 us (13%)
  other arithmetic  9.31 us (7%)
  local copies, waits for them, and re-layouts  2.76 us (2%)
    all_to_all x1, blocking collectives, local(): parts = lax.all_to_all(own.astype(bf16).reshape(NZ, per, d), 'z', 0, 0)  32.2 us
    all_to_all x1, waiting for transfers between devices, local(): packed = lax.all_to_all(packed, 'y', 0, 0)  27 us
    ppermute x3, starting transfers between devices, local(): g = [lax.ppermute(g0, 'x', shift(NX, -k)) for k in range(1, NX)]  14.5 us
    ppermute x3, waiting for transfers between devices, local(): lax.ppermute(sent[(k - 1) * blk:k * blk], 'x', shift(NX, k))  12.8 us
    pallas_call x1, Pallas kernels, local(): pl.pallas_call(main_kernel, name='main', in_specs=[VMEM, VMEM, VMEM, ANY,...  12.1 us
    ppermute x3, starting transfers between devices, local(): lax.ppermute(sent[(k - 1) * blk:k * blk], 'x', shift(NX, k))  7.76 us
    all_to_all x1, starting transfers between devices, local(): packed = lax.all_to_all(packed, 'y', 0, 0)  7.11 us
    ppermute x3, waiting for transfers between devices, local(): g = [lax.ppermute(g0, 'x', shift(NX, -k)) for k in range(1, NX)]  6.02 us
  transfers between devices with their start and end apart: 9, of which 5 were waited for; matrix products, arithmetic and copies ran while one was open for 6% of the time, Pallas kernels for 2%

profile of v1, /device:TPU:4, one launch (start us, length us, event | category | flops | bytes accessed | tf_op | source)
XLA Modules:
  0.0 142.5 jit_solution(17914984042982596313)
XLA Ops:
  0.6 0.8 fusion.18.order_ref
  1.5 12.1 %main.1 = (bf16[96,8192]{1,0:T(8,128)(2,1)}, bf16[96,8192]{1,0:T(8,128)(2,1)}) custom-call(s32[192,1]{1,0:T(8,128)} %fusion.18.order_ref, bf16[176,192]{1,0:T(8,128)(2,1)} %bitcast.11, bf16[176,192]{1,0:T(8,128)(2,1)} %bitcast.13, bf16[192,8192]{1,0:T(8,128)(2,1)} %grad_ref.1, bf16[176,8192]{1,0:T(8,128)(2,1)} %wd_hbm.1, bf16[176,8192]{1,0:T(8,128)(2,1)} %wg_hbm.1, ...), custom_call_target="tpu_custom_call" | custom-call | flops 1660944384 | bytes 14000000 | tf_op jit(solution)/shard_map/main/pallas_call | solution.py:177
  13.6 1.9 %collective-permute-start = (bf16[96,8192]{1,0:T(8,128)(2,1)}, bf16[96,8192]{1,0:T(8,128)(2,1)S(1)}, u32[]{:S(2)}, u32[]{:S(2)}) collective-permute-start(bf16[96,8192]{1,0:T(8,128)(2,1)} %get-tuple-element.5), channel_id=1, source_target_pairs={{0,1},{1,0},{2,3},{3,2},{4,5},{5,4},{6,7},{7,6},{8,9},{9,8},{10,11... | collective-permute-start | bytes 4718600 | tf_op jit(solution)/shard_map/ppermute | solution.py:193
  15.5 0.8 fusion.24.order_ref
  16.3 2.4 %pack.1 = bf16[8,288,256]{2,1,0:T(8,128)(2,1)} custom-call(s32[1]{0:T(128)} %bitcast.2.at_ref, s32[192,1]{1,0:T(8,128)} %fusion.24.order_ref, bf16[192,8192]{1,0:T(8,128)(2,1)} %grad_ref.1, bf16[176,192]{1,0:T(8,128)(2,1)} %bitcast.12, bf16[176,192]{1,0:T(8,128)(2,1)} %bitcast.14), custom_call_target="tpu_custom_call" | custom-call | flops 12976128 | bytes 2000000 | tf_op jit(solution)/shard_map/pack/pallas_call | solution.py:154
  18.7 7.1 %all-to-all-start.1 = ((bf16[8,288,256]{2,1,0:T(8,128)(2,1)}), bf16[8,288,256]{2,1,0:T(8,128)(2,1)S(1)}, u32[]{:S(2)}, u32[]{:S(2)}) async-start(bf16[8,288,256]{2,1,0:T(8,128)(2,1)} %pack.1), calls=%async_computation.1 | async-start | bytes 2359296 | tf_op jit(solution)/shard_map/all_to_all | solution.py:175
  25.8 0.0 collective-permute-done
  25.8 0.0 copy-start.5
  25.8 1.2 copy-done.5
  27.0 4.0 %fusion.30 = (bf16[96,8192]{1,0:T(8,128)(2,1)S(1)}, f32[96,8192]{1,0:T(8,128)}) fusion(bf16[96,8192]{1,0:T(8,128)(2,1)} %copy-done.5, bf16[96,8192]{1,0:T(8,128)(2,1)} %get-tuple-element.4), kind=kLoop, calls=%fused_computation.55 | loop fusion | flops 3145728 | bytes 7864320 | tf_op jit(solution)/shard_map/convert.1
  31.0 27.0 %all-to-all-done.1.own_ref = bf16[8,288,256]{2,1,0:T(8,128)(2,1)S(1)} async-done(((bf16[8,288,256]{2,1,0:T(8,128)(2,1)}), bf16[8,288,256]{2,1,0:T(8,128)(2,1)S(1)}, u32[]{:S(2)}, u32[]{:S(2)}) %all-to-all-start.1) | async-done | bytes 1179680 | tf_op jit(solution)/shard_map/all_to_all | solution.py:175
  58.0 0.0 copy-start
  58.0 0.1 slice_bitcast_fusion
  58.1 2.4 %collective-permute-start.4 = (bf16[8,96,256]{2,1,0:T(8,128)(2,1)S(1)}, bf16[8,96,256]{2,1,0:T(8,128)(2,1)S(1)}, u32[]{:S(2)}, u32[]{:S(2)}) collective-permute-start(bf16[8,96,256]{2,1,0:T(8,128)(2,1)S(1)} %get-tuple-element.12), channel_id=1, source_target_pairs={{0,6},{2,0},{4,2},{6,4},{1,7},{3,1},{5,3},{7,5},{8,14},{10,8},{12,... | collective-permute-start | bytes 1179656 | tf_op jit(solution)/shard_map/ppermute | solution.py:207
  60.5 7.5 %collective-permute-start.5 = (bf16[8,96,256]{2,1,0:T(8,128)(2,1)S(1)}, bf16[8,96,256]{2,1,0:T(8,128)(2,1)S(1)}, u32[]{:S(2)}, u32[]{:S(2)}) collective-permute-start(bf16[8,96,256]{2,1,0:T(8,128)(2,1)S(1)} %get-tuple-element.12), channel_id=1, source_target_pairs={{0,4},{2,6},{4,0},{6,2},{1,5},{3,7},{5,1},{7,3},{8,12},{10,14},{12... | collective-permute-start | bytes 1179656 | tf_op jit(solution)/shard_map/ppermute | solution.py:207
  68.1 4.5 %collective-permute-start.6 = (bf16[8,96,256]{2,1,0:T(8,128)(2,1)S(1)}, bf16[8,96,256]{2,1,0:T(8,128)(2,1)S(1)}, u32[]{:S(2)}, u32[]{:S(2)}) collective-permute-start(bf16[8,96,256]{2,1,0:T(8,128)(2,1)S(1)} %get-tuple-element.12), channel_id=1, source_target_pairs={{0,2},{2,4},{4,6},{6,0},{1,3},{3,5},{5,7},{7,1},{8,10},{10,12},{12... | collective-permute-start | bytes 1179656 | tf_op jit(solution)/shard_map/ppermute | solution.py:207
  72.6 0.1 fusion.31
  72.7 0.0 copy-done
  72.7 1.9 %collective-permute-start.3 = (bf16[24,8192]{1,0:T(8,128)(2,1)S(1)}, bf16[24,8192]{1,0:T(8,128)(2,1)S(1)}, u32[]{:S(2)}, u32[]{:S(2)}) collective-permute-start(bf16[24,8192]{1,0:T(8,128)(2,1)S(1)} %get-tuple-element.9), channel_id=1, source_target_pairs={{0,4},{2,6},{4,0},{6,2},{1,5},{3,7},{5,1},{7,3},{8,12},{10,14},{12... | collective-permute-start | bytes 1179656 | tf_op jit(solution)/shard_map/ppermute | solution.py:199
  74.7 3.4 %collective-permute-start.2 = (bf16[24,8192]{1,0:T(8,128)(2,1)S(1)}, bf16[24,8192]{1,0:T(8,128)(2,1)S(1)}, u32[]{:S(2)}, u32[]{:S(2)}) collective-permute-start(bf16[24,8192]{1,0:T(8,128)(2,1)S(1)} %get-tuple-element.10), channel_id=1, source_target_pairs={{0,6},{2,0},{4,2},{6,4},{1,7},{3,1},{5,3},{7,5},{8,14},{10,8},{12,... | collective-permute-start | bytes 1179656 | tf_op jit(solution)/shard_map/ppermute | solution.py:199
  78.0 0.0 collective-permute-done.4.x1_ref
  78.0 0.0 copy-start.1
  78.0 2.5 %collective-permute-start.1 = (bf16[24,8192]{1,0:T(8,128)(2,1)S(1)}, bf16[24,8192]{1,0:T(8,128)(2,1)S(1)}, u32[]{:S(2)}, u32[]{:S(2)}) collective-permute-start(bf16[24,8192]{1,0:T(8,128)(2,1)S(1)} %get-tuple-element.8), channel_id=1, source_target_pairs={{0,2},{2,4},{4,6},{6,0},{1,3},{3,5},{5,7},{7,1},{8,10},{10,12},{12... | collective-permute-start | bytes 1179656 | tf_op jit(solution)/shard_map/ppermute | solution.py:199
  80.5 0.0 collective-permute-done.5.x2_ref
  80.5 0.0 copy-start.2
  80.5 6.0 %collective-permute-done.6.x3_ref = bf16[8,96,256]{2,1,0:T(8,128)(2,1)S(1)} collective-permute-done((bf16[8,96,256]{2,1,0:T(8,128)(2,1)S(1)}, bf16[8,96,256]{2,1,0:T(8,128)(2,1)S(1)}, u32[]{:S(2)}, u32[]{:S(2)}) %collective-permute-start.6) | collective-permute-done | bytes 393248 | tf_op jit(solution)/shard_map/ppermute | solution.py:207
  86.6 0.0 copy-start.3
  86.6 1.4 pad_maximum_fusion
  87.9 0.0 copy-done.1
  87.9 0.0 copy-done.2
  87.9 0.0 copy-done.3
  87.9 1.9 %collective-permute-start.7 = (bf16[4,8,96,256]{3,2,1,0:T(8,128)(2,1)}, bf16[4,8,96,256]{3,2,1,0:T(8,128)(2,1)S(1)}, u32[]{:S(2)}, u32[]{:S(2)}) collective-permute-start(bf16[4,8,96,256]{3,2,1,0:T(8,128)(2,1)} %pad_maximum_fusion), channel_id=1, source_target_pairs={{0,1},{1,0},{2,3},{3,2},{4,5},{5,4},{6,7},{7,6},{8,9},{9,8},{10,11... | collective-permute-start | bytes 4718600 | tf_op jit(solution)/shard_map/ppermute | solution.py:208
  89.9 5.1 %collective-permute-done.3 = bf16[24,8192]{1,0:T(8,128)(2,1)S(1)} collective-permute-done((bf16[24,8192]{1,0:T(8,128)(2,1)S(1)}, bf16[24,8192]{1,0:T(8,128)(2,1)S(1)}, u32[]{:S(2)}, u32[]{:S(2)}) %collective-permute-start.3) | collective-permute-done | bytes 393248 | tf_op jit(solution)/shard_map/ppermute | solution.py:199
  95.0 1.4 collective-permute-done.2
  96.4 6.3 %collective-permute-done.1 = bf16[24,8192]{1,0:T(8,128)(2,1)S(1)} collective-permute-done((bf16[24,8192]{1,0:T(8,128)(2,1)S(1)}, bf16[24,8192]{1,0:T(8,128)(2,1)S(1)}, u32[]{:S(2)}, u32[]{:S(2)}) %collective-permute-start.1) | collective-permute-done | bytes 393248 | tf_op jit(solution)/shard_map/ppermute | solution.py:199
  102.7 1.3 fusion
  104.0 0.3 reshape.270
  104.3 32.2 %all_to_all.10 = bf16[12,2,8192]{2,1,0:T(2,128)(2,1)S(1)} all-to-all(bf16[12,2,8192]{2,1,0:T(2,128)(2,1)S(1)} %reshape.270), channel_id=1, replica_groups=mesh['y'=8,'z'=12,'x'=4,'c'=2] {'z'}, dimensions={0} | all-to-all | bytes 786432 | tf_op jit(solution)/shard_map/all_to_all | solution.py:203
  136.5 1.0 reduce_sum.12
  137.4 0.0 collective-permute-done.7.core_ref
  137.4 0.0 copy-start.4
  137.4 1.2 copy-done.4
  138.6 3.9 %down.1 = bf16[176,1024]{1,0:T(8,128)(2,1)} custom-call(bf16[8,288,256]{2,1,0:T(8,128)(2,1)} %copy-done, bf16[8,96,256]{2,1,0:T(8,128)(2,1)} %copy-done.1, bf16[8,96,256]{2,1,0:T(8,128)(2,1)} %copy-done.2, bf16[8,96,256]{2,1,0:T(8,128)(2,1)} %copy-done.3, bf16[4,8,96,256]{3,2,1,0:T(8,128)(2,1)} %copy-done.4), custom_call_target="tpu_custom_call" | custom-call | flops 553648128 | bytes 8000000 | tf_op jit(solution)/shard_map/down/pallas_call | solution.py:209
Async XLA Ops:
  13.6 12.2 %collective-permute-start = (bf16[96,8192]{1,0:T(8,128)(2,1)}, bf16[96,8192]{1,0:T(8,128)(2,1)S(1)}, u32[]{:S(2)}, u32[]{:S(2)}) collective-permute-start(bf16[96,8192]{1,0:T(8,128)(2,1)} %get-tuple-element.5), channel_id=1, source_target_pairs={{0,1},{1,0},{2,3},{3,2},{4,5},{5,4},{6,7},{7,6},{8,9},{9,8},{10,11... | collective-permute-start | bytes 4718600 | tf_op jit(solution)/shard_map/ppermute | solution.py:193
  18.7 39.4 %all-to-all-start.1 = ((bf16[8,288,256]{2,1,0:T(8,128)(2,1)}), bf16[8,288,256]{2,1,0:T(8,128)(2,1)S(1)}, u32[]{:S(2)}, u32[]{:S(2)}) async-start(bf16[8,288,256]{2,1,0:T(8,128)(2,1)} %pack.1), calls=%async_computation.1 | async-start | bytes 2359296 | tf_op jit(solution)/shard_map/all_to_all | solution.py:175
  25.8 1.2 copy-start.5
  58.0 14.7 %copy-start = (bf16[8,288,256]{2,1,0:T(8,128)(2,1)}, bf16[8,288,256]{2,1,0:T(8,128)(2,1)S(1)}, u32[]{:S(2)}) copy-start(bf16[8,288,256]{2,1,0:T(8,128)(2,1)S(1)} %all-to-all-done.1.own_ref) | copy-start | bytes 3538948
  58.1 19.9 %collective-permute-start.4 = (bf16[8,96,256]{2,1,0:T(8,128)(2,1)S(1)}, bf16[8,96,256]{2,1,0:T(8,128)(2,1)S(1)}, u32[]{:S(2)}, u32[]{:S(2)}) collective-permute-start(bf16[8,96,256]{2,1,0:T(8,128)(2,1)S(1)} %get-tuple-element.12), channel_id=1, source_target_pairs={{0,6},{2,0},{4,2},{6,4},{1,7},{3,1},{5,3},{7,5},{8,14},{10,8},{12,... | collective-permute-start | bytes 1179656 | tf_op jit(solution)/shard_map/ppermute | solution.py:207
  60.5 20.0 %collective-permute-start.5 = (bf16[8,96,256]{2,1,0:T(8,128)(2,1)S(1)}, bf16[8,96,256]{2,1,0:T(8,128)(2,1)S(1)}, u32[]{:S(2)}, u32[]{:S(2)}) collective-permute-start(bf16[8,96,256]{2,1,0:T(8,128)(2,1)S(1)} %get-tuple-element.12), channel_id=1, source_target_pairs={{0,4},{2,6},{4,0},{6,2},{1,5},{3,7},{5,1},{7,3},{8,12},{10,14},{12... | collective-permute-start | bytes 1179656 | tf_op jit(solution)/shard_map/ppermute | solution.py:207
  68.1 18.5 %collective-permute-start.6 = (bf16[8,96,256]{2,1,0:T(8,128)(2,1)S(1)}, bf16[8,96,256]{2,1,0:T(8,128)(2,1)S(1)}, u32[]{:S(2)}, u32[]{:S(2)}) collective-permute-start(bf16[8,96,256]{2,1,0:T(8,128)(2,1)S(1)} %get-tuple-element.12), channel_id=1, source_target_pairs={{0,2},{2,4},{4,6},{6,0},{1,3},{3,5},{5,7},{7,1},{8,10},{10,12},{12... | collective-permute-start | bytes 1179656 | tf_op jit(solution)/shard_map/ppermute | solution.py:207
  72.7 22.3 %collective-permute-start.3 = (bf16[24,8192]{1,0:T(8,128)(2,1)S(1)}, bf16[24,8192]{1,0:T(8,128)(2,1)S(1)}, u32[]{:S(2)}, u32[]{:S(2)}) collective-permute-start(bf16[24,8192]{1,0:T(8,128)(2,1)S(1)} %get-tuple-element.9), channel_id=1, source_target_pairs={{0,4},{2,6},{4,0},{6,2},{1,5},{3,7},{5,1},{7,3},{8,12},{10,14},{12... | collective-permute-start | bytes 1179656 | tf_op jit(solution)/shard_map/ppermute | solution.py:199
  74.7 21.7 %collective-permute-start.2 = (bf16[24,8192]{1,0:T(8,128)(2,1)S(1)}, bf16[24,8192]{1,0:T(8,128)(2,1)S(1)}, u32[]{:S(2)}, u32[]{:S(2)}) collective-permute-start(bf16[24,8192]{1,0:T(8,128)(2,1)S(1)} %get-tuple-element.10), channel_id=1, source_target_pairs={{0,6},{2,0},{4,2},{6,4},{1,7},{3,1},{5,3},{7,5},{8,14},{10,8},{12,... | collective-permute-start | bytes 1179656 | tf_op jit(solution)/shard_map/ppermute | solution.py:199
  78.0 9.9 %copy-start.1 = (bf16[8,96,256]{2,1,0:T(8,128)(2,1)}, bf16[8,96,256]{2,1,0:T(8,128)(2,1)S(1)}, u32[]{:S(2)}) copy-start(bf16[8,96,256]{2,1,0:T(8,128)(2,1)S(1)} %collective-permute-done.4.x1_ref) | copy-start | bytes 1179652
  78.0 24.7 %collective-permute-start.1 = (bf16[24,8192]{1,0:T(8,128)(2,1)S(1)}, bf16[24,8192]{1,0:T(8,128)(2,1)S(1)}, u32[]{:S(2)}, u32[]{:S(2)}) collective-permute-start(bf16[24,8192]{1,0:T(8,128)(2,1)S(1)} %get-tuple-element.8), channel_id=1, source_target_pairs={{0,2},{2,4},{4,6},{6,0},{1,3},{3,5},{5,7},{7,1},{8,10},{10,12},{12... | collective-permute-start | bytes 1179656 | tf_op jit(solution)/shard_map/ppermute | solution.py:199
  80.5 7.4 %copy-start.2 = (bf16[8,96,256]{2,1,0:T(8,128)(2,1)}, bf16[8,96,256]{2,1,0:T(8,128)(2,1)S(1)}, u32[]{:S(2)}) copy-start(bf16[8,96,256]{2,1,0:T(8,128)(2,1)S(1)} %collective-permute-done.5.x2_ref) | copy-start | bytes 1179652
  86.6 1.4 copy-start.3
  87.9 49.5 %collective-permute-start.7 = (bf16[4,8,96,256]{3,2,1,0:T(8,128)(2,1)}, bf16[4,8,96,256]{3,2,1,0:T(8,128)(2,1)S(1)}, u32[]{:S(2)}, u32[]{:S(2)}) collective-permute-start(bf16[4,8,96,256]{3,2,1,0:T(8,128)(2,1)} %pad_maximum_fusion), channel_id=1, source_target_pairs={{0,1},{1,0},{2,3},{3,2},{4,5},{5,4},{6,7},{7,6},{8,9},{9,8},{10,11... | collective-permute-start | bytes 4718600 | tf_op jit(solution)/shard_map/ppermute | solution.py:208
  137.4 1.2 copy-start.4
